TPU v7x, 32 devices: a whole 2x2x4 slice. The times are simulated.
32 devices in a mesh: grp: 2 (over x), seq: 8 (over z, y), rep: 2 (over core).
Axes of the slice: x: 2, y: 2, z: 4, core: 2. Of those that a mesh axis runs over, the one named last changes fastest.
Arguments:
- queries: bfloat16 [4, 2048, 1024], P(('grp', 'rep'), None, 'seq'), parts along dimension 0, may hold values from -60 to 60
- key_vectors: bfloat16 [4, 2048, 1024], P(('grp', 'rep'), None, 'seq'), parts along dimension 0, may hold values from -8 to 8
- value_vectors: bfloat16 [4, 2048, 1024], P(('grp', 'rep'), None, 'seq'), parts along dimension 0, may hold values from -6 to 6
- context: bfloat16 [4, 2048, 1024], P(('grp', 'rep'), None, 'seq'), parts along dimension 0, may hold values from -6 to 6
- cotangent: bfloat16 [4, 2048, 1024], P(('grp', 'rep'), None, 'seq'), parts along dimension 0, may hold values from -6 to 6
- out_weight: bfloat16 [4096, 2048], P('grp'), parts along dimension 0, may hold values from -0.125 to 0.125
- membership: int32 [4, 1024], P(('grp', 'rep'), 'seq'), parts along dimension 0, may hold values from 0 to 1, as said below
Outputs:
- grad_queries: bfloat16 [4, 2048, 1024], P(('grp', 'rep'), None, 'seq'), parts along dimension 0
- grad_keys: bfloat16 [4, 2048, 1024], P(('grp', 'rep'), None, 'seq'), parts along dimension 0
- grad_values: bfloat16 [4, 2048, 1024], P(('grp', 'rep'), None, 'seq'), parts along dimension 0
- grad_weight: float32 [4096, 2048], P(('grp', 'seq', 'rep')), parts along dimension 0
There are 2 independent parts, one for each index of `grp`. A program takes and returns all parts, laid end to end along the dimension named above; each array names one. Nothing has to cross between parts.
Inputs may be any that keep to these rules, and one draw needn't show every extreme that they name: Every window has at least one cell with membership 1.
All inputs are finite; a program needn't handle non-finite values.
Results may differ from a plain program's by a relative error of at most 0.0058.
Values may be sent and summed in bfloat16 or wider, within the bound.
A program may use at most 128 MiB of HBM per device.

v0:
```python
import math

import jax
import jax.numpy as jnp
from jax import lax
from jax.sharding import PartitionSpec as P

DH = 64


def contract_cells(left_rows, right_rows):
    return lax.dot_general(
        left_rows, right_rows, (((1,), (1,)), ((), ())), preferred_element_type=jnp.float32
    )


def attention_grads(query_heads, key_heads, value_heads, grad_heads, context_heads, member_keys):
    score_scale = 1.0 / math.sqrt(DH)
    length = key_heads.shape[2]
    block_rows = min(512, length)
    block_count = length // block_rows

    def one_block(block_index, carry):
        key_total, value_total, query_grads = carry
        first = block_index * block_rows
        query_block = lax.dynamic_slice_in_dim(query_heads, first, block_rows, 2)
        grad_block = lax.dynamic_slice_in_dim(grad_heads, first, block_rows, 2)
        context_block = lax.dynamic_slice_in_dim(context_heads, first, block_rows, 2)
        scores = (
            jnp.einsum("hdq,hdk->hqk", query_block, key_heads, preferred_element_type=jnp.float32)
            * score_scale
        )
        scores = jnp.where(member_keys[None, None, :], scores, -jnp.inf)
        highest = jnp.max(scores, axis=2, keepdims=True)
        exp_scores = jnp.exp(scores - highest)
        probabilities = exp_scores / jnp.sum(exp_scores, axis=2, keepdims=True)
        row_delta = jnp.sum(
            grad_block.astype(jnp.float32) * context_block.astype(jnp.float32), axis=1
        )
        probs_low = probabilities.astype(jnp.bfloat16)
        value_total = value_total + jnp.einsum(
            "hdq,hqk->hdk", grad_block, probs_low, preferred_element_type=jnp.float32
        )
        grad_probs = jnp.einsum(
            "hdq,hdk->hqk", grad_block, value_heads, preferred_element_type=jnp.float32
        )
        grad_scores = (probabilities * (grad_probs - row_delta[:, :, None]) * score_scale).astype(
            jnp.bfloat16
        )
        query_block_grad = jnp.einsum(
            "hdk,hqk->hdq", key_heads, grad_scores, preferred_element_type=jnp.float32
        ).astype(jnp.bfloat16)
        key_total = key_total + jnp.einsum(
            "hdq,hqk->hdk", query_block, grad_scores, preferred_element_type=jnp.float32
        )
        query_grads = lax.dynamic_update_slice_in_dim(query_grads, query_block_grad, first, 2)
        return (key_total, value_total, query_grads)

    start_state = (
        jnp.zeros(key_heads.shape, jnp.float32),
        jnp.zeros(key_heads.shape, jnp.float32),
        jnp.zeros(key_heads.shape, jnp.bfloat16),
    )
    key_total, value_total, query_grads = lax.fori_loop(0, block_count, one_block, start_state)
    return (query_grads, key_total.astype(jnp.bfloat16), value_total.astype(jnp.bfloat16))


def on_device(queries, key_vectors, value_vectors, context, cotangent, out_weight, membership):
    query_local = queries[0]
    key_local = key_vectors[0]
    value_local = value_vectors[0]
    context_local = context[0]
    cotangent_local = cotangent[0]
    flags_all = lax.all_gather(membership, "seq", axis=1, tiled=True)[0]
    member_keys = flags_all > 0
    grad_context = jnp.dot(out_weight, cotangent_local, preferred_element_type=jnp.float32).astype(
        jnp.bfloat16
    )
    query_cols, key_cols, value_cols, grad_cols, context_cols = (
        lax.all_to_all(query_local, "seq", split_axis=0, concat_axis=1, tiled=True),
        lax.all_to_all(key_local, "seq", split_axis=0, concat_axis=1, tiled=True),
        lax.all_to_all(value_local, "seq", split_axis=0, concat_axis=1, tiled=True),
        lax.all_to_all(grad_context, "seq", split_axis=0, concat_axis=1, tiled=True),
        lax.all_to_all(context_local, "seq", split_axis=0, concat_axis=1, tiled=True),
    )
    head_count = query_cols.shape[0] // DH
    length = query_cols.shape[1]
    shaped = [
        array.reshape(head_count, DH, length)
        for array in (query_cols, key_cols, value_cols, grad_cols, context_cols)
    ]
    query_grads, key_grads, value_grads = attention_grads(
        shaped[0], shaped[1], shaped[2], shaped[3], shaped[4], member_keys
    )
    grad_query, grad_key, grad_value = (
        lax.all_to_all(
            query_grads.reshape(head_count * DH, length),
            "seq",
            split_axis=1,
            concat_axis=0,
            tiled=True,
        ),
        lax.all_to_all(
            key_grads.reshape(head_count * DH, length),
            "seq",
            split_axis=1,
            concat_axis=0,
            tiled=True,
        ),
        lax.all_to_all(
            value_grads.reshape(head_count * DH, length),
            "seq",
            split_axis=1,
            concat_axis=0,
            tiled=True,
        ),
    )
    grad_weight = lax.psum_scatter(
        contract_cells(context_local, cotangent_local),
        ("seq", "rep"),
        scatter_dimension=0,
        tiled=True,
    )
    return (grad_query[None], grad_key[None], grad_value[None], grad_weight)


def solution(mesh):
    placed = (
        P(("grp", "rep"), None, "seq"),
        P(("grp", "rep"), None, "seq"),
        P(("grp", "rep"), None, "seq"),
        P(("grp", "rep"), None, "seq"),
        P(("grp", "rep"), None, "seq"),
        P("grp", None),
        P(("grp", "rep"), "seq"),
    )
    return jax.shard_map(
        on_device,
        mesh=mesh,
        in_specs=placed,
        out_specs=(
            P(("grp", "rep"), None, "seq"),
            P(("grp", "rep"), None, "seq"),
            P(("grp", "rep"), None, "seq"),
            P(("grp", "seq", "rep"), None),
        ),
        check_vma=False,
    )
```

profile of v0, /device:TPU:0, one launch (start us, length us, event | category | flops | bytes accessed | tf_op | source)
XLA Modules:
  0.0 287.0 jit_solution(17907125019709560862)
XLA Ops:
  7.2 1.0 copy-done
  8.2 9.1 %fusion.33 = f32[2048,2048]{1,0:T(8,128)} fusion(bf16[1,2048,128]{2,1,0:T(8,128)(2,1)} %param.12, bf16[1,2048,128]{2,1,0:T(8,128)(2,1)S(1)} %copy-done), kind=kOutput, calls=%fused_computation.32 | convolution fusion | flops 1073741824 | bytes 17825792 | tf_op jit(solution)/shard_map/dot_general | solution.py:12
  17.4 1.0 copy-done.5
  18.4 21.6 %all_to_all.128 = bf16[8,256,128]{2,1,0:T(8,128)(2,1)S(1)} all-to-all(bf16[8,256,128]{2,1,0:T(8,128)(2,1)S(1)} %bitcast.72), channel_id=1, replica_groups=mesh['grp'=2,'seq'=8,'rep'=2] {'seq'}, dimensions={0} | all-to-all | bytes 1048576 | tf_op jit(solution)/shard_map/all_to_all | solution.py:80
  40.0 17.5 %all_to_all.129 = bf16[8,256,128]{2,1,0:T(8,128)(2,1)S(1)} all-to-all(bf16[8,256,128]{2,1,0:T(8,128)(2,1)S(1)} %bitcast.73), channel_id=1, replica_groups=mesh['grp'=2,'seq'=8,'rep'=2] {'seq'}, dimensions={0} | all-to-all | bytes 1048576 | tf_op jit(solution)/shard_map/all_to_all | solution.py:81
  57.5 33.3 %all_to_all.130 = bf16[8,256,128]{2,1,0:T(8,128)(2,1)} all-to-all(bf16[8,256,128]{2,1,0:T(8,128)(2,1)S(1)} %bitcast.74), channel_id=1, replica_groups=mesh['grp'=2,'seq'=8,'rep'=2] {'seq'}, dimensions={0} | all-to-all | bytes 1048576 | tf_op jit(solution)/shard_map/all_to_all | solution.py:82
  90.8 3.5 %all-to-all-start.4 = ((bf16[8,256,128]{2,1,0:T(8,128)(2,1)}), bf16[8,256,128]{2,1,0:T(8,128)(2,1)S(1)}, u32[]{:S(2)}, u32[]{:S(2)}) async-start(bf16[8,256,128]{2,1,0:T(8,128)(2,1)} %bitcast.9), calls=%async_computation.4 | async-start | bytes 1048576 | tf_op jit(solution)/shard_map/all_to_all | solution.py:84
  94.3 6.6 %convolution_convert_fusion.1 = bf16[2048,128]{1,0:T(8,128)(2,1)} fusion(bf16[2048,2048]{1,0:T(8,128)(2,1)} %param.14, bf16[1,2048,128]{2,1,0:T(8,128)(2,1)S(1)} %copy-done), kind=kOutput, calls=%fused_computation.31 | convolution fusion | flops 1074003968 | bytes 9437184 | tf_op jit(solution)/shard_map/dot_general | solution.py:76
  100.9 20.7 %all-to-all-done.4 = bf16[8,256,128]{2,1,0:T(8,128)(2,1)S(1)} async-done(((bf16[8,256,128]{2,1,0:T(8,128)(2,1)}), bf16[8,256,128]{2,1,0:T(8,128)(2,1)S(1)}, u32[]{:S(2)}, u32[]{:S(2)}) %all-to-all-start.4) | async-done | bytes 524320 | tf_op jit(solution)/shard_map/all_to_all | solution.py:84
  121.6 4.1 %all-to-all-start.2 = ((bf16[8,256,128]{2,1,0:T(8,128)(2,1)}), bf16[8,256,128]{2,1,0:T(8,128)(2,1)}, u32[]{:S(2)}, u32[]{:S(2)}) async-start(bf16[8,256,128]{2,1,0:T(8,128)(2,1)} %bitcast.5), calls=%async_computation.2 | async-start | bytes 1048576 | tf_op jit(solution)/shard_map/all_to_all | solution.py:83
  125.8 32.0 %all_gather.3 = s32[1,1024]{1,0:T(1,128)S(1)} all-gather(s32[1,128]{1,0:T(1,128)S(1)} %copy-done.9), channel_id=1, replica_groups=mesh['grp'=2,'seq'=8,'rep'=2] {'seq'}, dimensions={1}, use_global_device_ids=true | all-gather | bytes 4608 | tf_op jit(solution)/shard_map/all_gather | solution.py:74
  157.8 1.1 copy.23
  159.0 1.3 reshape.71
  160.2 1.1 copy.24
  161.4 1.3 reshape.72
  162.6 2.2 copy.26
  164.8 2.1 reshape.74
  166.9 1.1 copy.27
  168.0 1.3 reshape.75
  169.3 2.2 copy.25
  171.5 2.1 reshape.73
  173.5 0.9 broadcast_in_dim.48
  174.4 34.2 %while.18 = (s32[]{:T(128)}, f32[4,64,1024]{2,1,0:T(8,128)S(1)}, f32[4,64,1024]{2,1,0:T(8,128)}, bf16[4,64,1024]{2,1,0:T(8,128)(2,1)}, bf16[4,64,1024]{2,1,0:T(8...) while((s32[]{:T(128)}, f32[4,64,1024]{2,1,0:T(8,128)S(1)}, ...), condition=%wide.region_4.5_spmd.clone, body=%wide.region_0.4_spmd.clone.sunk | while | flops 1366948864 | bytes 87336304 | solution.py:64
  174.4 1.1 multiply_reduce_fusion.2
  175.5 4.8 %fusion.72 = (f32[4,512]{1,0:T(4,128)S(1)}, f32[4,512,1024]{2,1,0:T(8,128)}) fusion(pred[1024]{0:T(1024)(128)(4,1)S(1)} %get-tuple-element.331, bf16[4,64,1024]{2,1,0:T(8,128)(2,1)S(1)} %get-tuple-element.332, bf16[4,64,1024]{2,1,0:T(8,128)(2,1)S(1)} %get-tuple-element.330, s32[]{:T(128)S(6)} %select_n.33), kind=kOutput, calls=%fused_computation.37.clone.1 | convolution fusion | flops 276825088 | bytes 9184260 | tf_op jit(solution)/shard_map/while/body/eval_jaxpr/sub | solution.py:35
  180.3 5.6 %fusion.73 = f32[4,64,1024]{2,1,0:T(8,128)} fusion(f32[4,512,1024]{2,1,0:T(8,128)} %get-tuple-element.296, f32[4,512]{1,0:T(4,128)S(1)} %get-tuple-element.297, f32[4,64,1024]{2,1,0:T(8,128)} %get-tuple-element.314, pred[]{:T(512)S(6)} %compare.3, bf16[4,64,1024]{2,1,0:T(8,128)(2,1)} %get-tuple-element.333, s32[]{:T(128)S(6)} %select_n.33), kind=kOutput, calls=%fused_computation.12.clone.1 | convolution fusion | flops 273154048 | bytes 10756101 | tf_op jit(solution)/shard_map/while/body/eval_jaxpr/hdq,hqk->hdk/dot_general | solution.py:41
  185.9 0.9 copy-done.10
  186.8 2.0 multiply_convert_fusion.2
  188.9 1.4 fusion.74
  190.3 1.0 convolution_add_fusion.2
  191.3 1.1 multiply_reduce_fusion.2
  192.4 4.8 %fusion.72 = (f32[4,512]{1,0:T(4,128)S(1)}, f32[4,512,1024]{2,1,0:T(8,128)}) fusion(pred[1024]{0:T(1024)(128)(4,1)S(1)} %get-tuple-element.331, bf16[4,64,1024]{2,1,0:T(8,128)(2,1)S(1)} %get-tuple-element.332, bf16[4,64,1024]{2,1,0:T(8,128)(2,1)S(1)} %get-tuple-element.330, s32[]{:T(128)S(6)} %select_n.33), kind=kOutput, calls=%fused_computation.37.clone.1 | convolution fusion | flops 276825088 | bytes 9184260 | tf_op jit(solution)/shard_map/while/body/eval_jaxpr/sub | solution.py:35
  197.2 5.9 %fusion.73 = f32[4,64,1024]{2,1,0:T(8,128)} fusion(f32[4,512,1024]{2,1,0:T(8,128)} %get-tuple-element.296, f32[4,512]{1,0:T(4,128)S(1)} %get-tuple-element.297, f32[4,64,1024]{2,1,0:T(8,128)} %get-tuple-element.314, pred[]{:T(512)S(6)} %compare.3, bf16[4,64,1024]{2,1,0:T(8,128)(2,1)} %get-tuple-element.333, s32[]{:T(128)S(6)} %select_n.33), kind=kOutput, calls=%fused_computation.12.clone.1 | convolution fusion | flops 273154048 | bytes 10756101 | tf_op jit(solution)/shard_map/while/body/eval_jaxpr/hdq,hqk->hdk/dot_general | solution.py:41
  203.1 1.0 copy-done.10
  204.1 2.0 multiply_convert_fusion.2
  206.2 1.4 fusion.74
  207.6 1.0 convolution_add_fusion.2
  208.6 1.2 copy.31
  209.8 0.9 copy.28
  210.7 8.3 %all-to-all-start.5 = ((bf16[256,8,128]{2,0,1:T(8,128)(2,1)}), bf16[256,8,128]{2,0,1:T(8,128)(2,1)S(1)}, u32[]{:S(2)}, u32[]{:S(2)}) async-start(bf16[256,8,128]{2,0,1:T(8,128)(2,1)} %copy.28), calls=%async_computation.5 | async-start | bytes 1048576 | tf_op jit(solution)/shard_map/all_to_all | solution.py:96
  219.2 0.9 copy.29
  220.0 22.3 %all-to-all-done.5 = bf16[256,8,128]{2,0,1:T(8,128)(2,1)S(1)} async-done(((bf16[256,8,128]{2,0,1:T(8,128)(2,1)}), bf16[256,8,128]{2,0,1:T(8,128)(2,1)S(1)}, u32[]{:S(2)}, u32[]{:S(2)}) %all-to-all-start.5) | async-done | bytes 524320 | tf_op jit(solution)/shard_map/all_to_all | solution.py:96
  242.4 3.7 %all-to-all-start.6 = ((bf16[256,8,128]{2,0,1:T(8,128)(2,1)}), bf16[256,8,128]{2,0,1:T(8,128)(2,1)S(1)}, u32[]{:S(2)}, u32[]{:S(2)}) async-start(bf16[256,8,128]{2,0,1:T(8,128)(2,1)} %copy.29), calls=%async_computation.6 | async-start | bytes 1048576 | tf_op jit(solution)/shard_map/all_to_all | solution.py:103
  246.3 0.9 copy.30
  247.2 12.9 %all-to-all-done.6 = bf16[256,8,128]{2,0,1:T(8,128)(2,1)S(1)} async-done(((bf16[256,8,128]{2,0,1:T(8,128)(2,1)}), bf16[256,8,128]{2,0,1:T(8,128)(2,1)S(1)}, u32[]{:S(2)}, u32[]{:S(2)}) %all-to-all-start.6) | async-done | bytes 524320 | tf_op jit(solution)/shard_map/all_to_all | solution.py:103
  260.1 3.6 %all-to-all-start.7 = ((bf16[256,8,128]{2,0,1:T(8,128)(2,1)}), bf16[256,8,128]{2,0,1:T(8,128)(2,1)S(1)}, u32[]{:S(2)}, u32[]{:S(2)}) async-start(bf16[256,8,128]{2,0,1:T(8,128)(2,1)} %copy.30), calls=%async_computation.7 | async-start | bytes 1048576 | tf_op jit(solution)/shard_map/all_to_all | solution.py:110
  263.7 14.2 %all-to-all-done.7 = bf16[256,8,128]{2,0,1:T(8,128)(2,1)S(1)} async-done(((bf16[256,8,128]{2,0,1:T(8,128)(2,1)}), bf16[256,8,128]{2,0,1:T(8,128)(2,1)S(1)}, u32[]{:S(2)}, u32[]{:S(2)}) %all-to-all-start.7) | async-done | bytes 524320 | tf_op jit(solution)/shard_map/all_to_all | solution.py:110
  277.8 0.8 copy.50
  (41 shorter events, 2.1 us)
Async XLA Ops:
  7.2 1.0 copy-start
  7.2 270.6 %reduce-scatter.2.cloned.1.call-start = ((), (), s32[]{:S(2)}) async-start(), calls=%async_computation.9 | async-start | bytes 17825792 | tf_op jit(solution)/shard_map/reduce_scatter | solution.py:118
  17.3 1.0 copy-start.5
  17.3 22.6 %copy-start.6 = (bf16[1,2048,128]{2,1,0:T(8,128)(2,1)S(1)}, bf16[1,2048,128]{2,1,0:T(8,128)(2,1)}, u32[]{:S(2)}) copy-start(bf16[1,2048,128]{2,1,0:T(8,128)(2,1)} %param.10) | copy-start | bytes 1572868
  17.3 40.2 %copy-start.7 = (bf16[1,2048,128]{2,1,0:T(8,128)(2,1)S(1)}, bf16[1,2048,128]{2,1,0:T(8,128)(2,1)}, u32[]{:S(2)}) copy-start(bf16[1,2048,128]{2,1,0:T(8,128)(2,1)} %param.11) | copy-start | bytes 1572868
  57.5 68.3 %copy-start.9 = (s32[1,128]{1,0:T(1,128)S(1)}, s32[1,128]{1,0:T(1,128)}, u32[]{:S(2)}) copy-start(s32[1,128]{1,0:T(1,128)} %param.15) | copy-start | bytes 1540
  90.8 30.8 %all-to-all-start.4 = ((bf16[8,256,128]{2,1,0:T(8,128)(2,1)}), bf16[8,256,128]{2,1,0:T(8,128)(2,1)S(1)}, u32[]{:S(2)}, u32[]{:S(2)}) async-start(bf16[8,256,128]{2,1,0:T(8,128)(2,1)} %bitcast.9), calls=%async_computation.4 | async-start | bytes 1048576 | tf_op jit(solution)/shard_map/all_to_all | solution.py:84
  121.6 47.7 %all-to-all-start.2 = ((bf16[8,256,128]{2,1,0:T(8,128)(2,1)}), bf16[8,256,128]{2,1,0:T(8,128)(2,1)}, u32[]{:S(2)}, u32[]{:S(2)}) async-start(bf16[8,256,128]{2,1,0:T(8,128)(2,1)} %bitcast.5), calls=%async_computation.2 | async-start | bytes 1048576 | tf_op jit(solution)/shard_map/all_to_all | solution.py:83
  180.3 5.7 %copy-start.1 = (bf16[4,64,1024]{2,1,0:T(8,128)(2,1)S(1)}, bf16[4,64,1024]{2,1,0:T(8,128)(2,1)}, u32[]{:S(2)}) copy-start(bf16[4,64,1024]{2,1,0:T(8,128)(2,1)} %get-tuple-element.333) | copy-start | bytes 1572868 | tf_op jit(solution)/shard_map/while
  180.3 5.7 %copy-start.8 = (bf16[4,64,1024]{2,1,0:T(8,128)(2,1)S(1)}, bf16[4,64,1024]{2,1,0:T(8,128)(2,1)}, u32[]{:S(2)}) copy-start(bf16[4,64,1024]{2,1,0:T(8,128)(2,1)} %get-tuple-element.334) | copy-start | bytes 1572868 | tf_op jit(solution)/shard_map/while
  180.3 6.6 %copy-start.10 = (f32[4,512,1024]{2,1,0:T(8,128)S(1)}, f32[4,512,1024]{2,1,0:T(8,128)}, u32[]{:S(2)}) copy-start(f32[4,512,1024]{2,1,0:T(8,128)} %get-tuple-element.296) | copy-start | bytes 25165828 | tf_op jit(solution)/shard_map/while
  186.8 2.0 copy-start.2
  190.3 1.0 copy-start.3
  197.2 5.9 %copy-start.1 = (bf16[4,64,1024]{2,1,0:T(8,128)(2,1)S(1)}, bf16[4,64,1024]{2,1,0:T(8,128)(2,1)}, u32[]{:S(2)}) copy-start(bf16[4,64,1024]{2,1,0:T(8,128)(2,1)} %get-tuple-element.333) | copy-start | bytes 1572868 | tf_op jit(solution)/shard_map/while
  197.2 5.9 %copy-start.8 = (bf16[4,64,1024]{2,1,0:T(8,128)(2,1)S(1)}, bf16[4,64,1024]{2,1,0:T(8,128)(2,1)}, u32[]{:S(2)}) copy-start(bf16[4,64,1024]{2,1,0:T(8,128)(2,1)} %get-tuple-element.334) | copy-start | bytes 1572868 | tf_op jit(solution)/shard_map/while
  197.2 6.9 %copy-start.10 = (f32[4,512,1024]{2,1,0:T(8,128)S(1)}, f32[4,512,1024]{2,1,0:T(8,128)}, u32[]{:S(2)}) copy-start(f32[4,512,1024]{2,1,0:T(8,128)} %get-tuple-element.296) | copy-start | bytes 25165828 | tf_op jit(solution)/shard_map/while
  204.1 2.1 copy-start.2
  207.6 1.0 copy-start.3
  208.6 37.6 %copy-start.4 = (f32[4,64,1024]{2,1,0:T(8,128)S(1)}, f32[4,64,1024]{2,1,0:T(8,128)}, u32[]{:S(2)}) copy-start(f32[4,64,1024]{2,1,0:T(8,128)} %get-tuple-element.177) | copy-start | bytes 3145732
  210.7 31.7 %all-to-all-start.5 = ((bf16[256,8,128]{2,0,1:T(8,128)(2,1)}), bf16[256,8,128]{2,0,1:T(8,128)(2,1)S(1)}, u32[]{:S(2)}, u32[]{:S(2)}) async-start(bf16[256,8,128]{2,0,1:T(8,128)(2,1)} %copy.28), calls=%async_computation.5 | async-start | bytes 1048576 | tf_op jit(solution)/shard_map/all_to_all | solution.py:96
  242.4 17.7 %all-to-all-start.6 = ((bf16[256,8,128]{2,0,1:T(8,128)(2,1)}), bf16[256,8,128]{2,0,1:T(8,128)(2,1)S(1)}, u32[]{:S(2)}, u32[]{:S(2)}) async-start(bf16[256,8,128]{2,0,1:T(8,128)(2,1)} %copy.29), calls=%async_computation.6 | async-start | bytes 1048576 | tf_op jit(solution)/shard_map/all_to_all | solution.py:103
  260.1 17.8 %all-to-all-start.7 = ((bf16[256,8,128]{2,0,1:T(8,128)(2,1)}), bf16[256,8,128]{2,0,1:T(8,128)(2,1)S(1)}, u32[]{:S(2)}, u32[]{:S(2)}) async-start(bf16[256,8,128]{2,0,1:T(8,128)(2,1)} %copy.30), calls=%async_computation.7 | async-start | bytes 1048576 | tf_op jit(solution)/shard_map/all_to_all | solution.py:110
Sparse Core Ops, SparseCore 0:
  17.5 225.5 reduce-scatter.1
where the time goes:
time: 288 us; the launch traced here: 287 us
  blocking collectives  104 us (36%)
  waiting for transfers between devices  70 us (24%)
  matrix products  45.7 us (16%)
  local copies, waits for them, and re-layouts  27 us (9%)
  starting transfers between devices  23.3 us (8%)
  between operations  14.2 us (5%)
    all_to_all x1, blocking collectives, on_device(): lax.all_to_all(value_local, 'seq', split_axis=0, concat_axis=1, tiled=True)  33.3 us
    all_gather x1, blocking collectives, on_device(): flags_all = lax.all_gather(membership, 'seq', axis=1, tiled=True)[0]  32 us
    all_to_all x1, waiting for transfers between devices, on_device(): lax.all_to_all(query_grads.reshape(head_count * DH, length), 'seq', split...  22.3 us
    all_to_all x1, blocking collectives, on_device(): lax.all_to_all(query_local, 'seq', split_axis=0, concat_axis=1, tiled=True)  21.6 us
    all_to_all x1, waiting for transfers between devices, on_device(): lax.all_to_all(context_local, 'seq', split_axis=0, concat_axis=1, tiled=T...  20.7 us
    all_to_all x1, blocking collectives, on_device(): lax.all_to_all(key_local, 'seq', split_axis=0, concat_axis=1, tiled=True)  17.5 us
    all_to_all x1, waiting for transfers between devices, on_device(): lax.all_to_all(value_grads.reshape(head_count * DH, length), 'seq', split...  14.2 us
    all_to_all x1, waiting for transfers between devices, on_device(): lax.all_to_all(key_grads.reshape(head_count * DH, length), 'seq', split_a...  12.9 us
  transfers between devices with their start and end apart: 6, of which 4 were waited for; matrix products, arithmetic and copies ran while one was open for 21% of the time, Pallas kernels for 0%

commit v1 on v0

v1 whole, which is shorter than its diff:
```python
import functools
import math

import jax
import jax.numpy as jnp
from jax import lax
from jax.experimental import pallas as pl
from jax.experimental.pallas import tpu as pltpu
from jax.sharding import PartitionSpec as P

DH = 64
MESH = pl.DeviceIdType.MESH
CHUNKS = 2


def kernel(n, ny, *refs):
    (q_ref, k_ref, v_ref, c_ref, cot_ref, w_ref, m_ref,
     dq_out, dk_out, dv_out, gw_out,
     q_buf, k_buf, v_buf, c_buf, g_buf, dq_buf, dk_buf, dv_buf,
     cot, w_buf, m_buf, gw, gw_in, k_acc, v_acc,
     w_sem, own_sem, m_send, m_recv, in_send, in_recv,
     ag_send, ag_recv, out_send, out_recv, gw_send, gw_recv) = refs
    me = lax.axis_index("seq")
    rep = lax.axis_index("rep")
    nz = n // ny
    z, y = me // ny, me % ny
    rows, length = q_buf.shape
    cells = length // n
    features = cot.shape[0]
    heads = rows // DH
    half = rows // 2
    piece = features // CHUNKS
    inputs = ((k_ref, k_buf), (q_ref, q_buf), (v_ref, v_buf), (c_ref, c_buf))
    outputs = ((dv_buf, dv_out), (dq_buf, dq_out), (dk_buf, dk_out))

    def cols(seq):
        return pl.ds(pl.multiple_of(seq * cells, cells), cells)

    def head_rows(h, owner=0):
        return pl.ds(pl.multiple_of(owner * rows + h * DH, DH), DH)

    barrier = pltpu.get_barrier_semaphore()
    for k in range(1, n):
        pl.semaphore_signal(barrier, inc=1, device_id={"seq": (me + k) % n}, device_id_type=MESH)
    pl.semaphore_signal(barrier, inc=1, device_id={"rep": 1 - rep}, device_id_type=MESH)

    w_copy = pltpu.make_async_copy(
        w_ref.at[pl.ds(pl.multiple_of(me * rows, rows), rows), :], w_buf, w_sem
    )
    w_copy.start()
    own_copy = pltpu.make_async_copy(cot_ref.at[0], cot.at[:, cols(me)], own_sem)
    own_copy.start()
    pltpu.make_async_copy(m_ref, m_buf.at[:, cols(me)], m_recv).start()

    pl.semaphore_wait(barrier, n)

    def ag_copy(step, part, origin, way, target):
        part_rows = pl.ds(part * piece, piece)
        landing = cot.at[part_rows, cols(origin)]
        source = cot_ref.at[0, part_rows, :] if step == 0 else landing
        return pltpu.make_async_remote_copy(
            src_ref=source,
            dst_ref=landing,
            send_sem=ag_send.at[way, step, part],
            recv_sem=ag_recv.at[part, origin],
            device_id={"seq": target},
            device_id_type=MESH,
        )

    def ag_wait(part, origin):
        landing = cot.at[pl.ds(part * piece, piece), cols(origin)]
        pltpu.make_async_copy(landing, landing, ag_recv.at[part, origin]).wait()

    def ag_step(step, arrived, send):
        for part in range(CHUNKS):
            up, down = z - step, z + step

            def act(origin, way, target):
                copy = ag_copy(step, part, origin, way, target)
                if send:
                    copy.start()
                else:
                    copy.wait_send()

            def cross(origin, way):
                if ny == 2:
                    act(origin, way, z * ny + 1 - y)

            @pl.when(up >= 0)
            def _():
                if arrived:
                    ag_wait(part, up * ny + y)

                @pl.when(z + 1 < nz)
                def _():
                    act(up * ny + y, 0, me + ny)

                cross(up * ny + y, 2)

            @pl.when(down < nz)
            def _():
                if arrived:
                    ag_wait(part, down * ny + y)

                @pl.when(z >= 1)
                def _():
                    act(down * ny + y, 1, me - ny)

                if step > 0:
                    cross(down * ny + y, 3)

    def send_inputs(h):
        for t, (ref, buf) in enumerate(inputs):
            pltpu.make_async_copy(
                ref.at[0, head_rows(h, me), :], buf.at[head_rows(h), cols(me)], in_recv.at[t, h]
            ).start()

        def to_peer(k, carry):
            peer = (me + k) % n
            for t, (ref, buf) in enumerate(inputs):
                pltpu.make_async_remote_copy(
                    src_ref=ref.at[0, head_rows(h, peer), :],
                    dst_ref=buf.at[head_rows(h), cols(me)],
                    send_sem=in_send.at[t],
                    recv_sem=in_recv.at[t, h],
                    device_id={"seq": peer},
                    device_id_type=MESH,
                ).start()
            return carry

        lax.fori_loop(1, n, to_peer, 0)

    def send_members(k, carry):
        pltpu.make_async_remote_copy(
            src_ref=m_ref,
            dst_ref=m_buf.at[:, cols(me)],
            send_sem=m_send,
            recv_sem=m_recv,
            device_id={"seq": (me + k) % n},
            device_id_type=MESH,
        ).start()
        return carry

    sent = 0
    for step in range(nz):
        ag_step(step, arrived=step > 0, send=True)
        if step == 0:
            lax.fori_loop(1, n, send_members, 0)
        upto = -(-(step + 1) * heads // nz)
        for h in range(sent, upto):
            send_inputs(h)
        sent = upto
    if ny == 2:
        for origin_z in range(nz):
            for part in range(CHUNKS):
                ag_wait(part, origin_z * ny + 1 - y)
    own_copy.wait()
    w_copy.wait()

    block = min(256, length)

    def project(i, carry):
        at = pl.ds(pl.multiple_of(i * block, block), block)
        g_buf[:, at] = jnp.dot(
            w_buf[...], cot[:, at], preferred_element_type=jnp.float32
        ).astype(jnp.bfloat16)
        return carry

    lax.fori_loop(0, length // block, project, 0)
    pltpu.make_async_copy(m_buf, m_buf, m_recv).wait()

    scale = 1.0 / math.sqrt(DH)
    tile = 256 if length <= 2048 else 128

    def one_head(h, carry):
        mine = head_rows(h)
        for t, (_, buf) in enumerate(inputs):
            pltpu.make_async_copy(buf.at[mine], buf.at[mine], in_recv.at[t, h]).wait()
        member = m_buf[...] > 0
        keys = k_buf[mine, :]
        values = v_buf[mine, :]
        keys_scaled = keys * jnp.bfloat16(scale)
        k_acc[...] = jnp.zeros_like(k_acc)
        v_acc[...] = jnp.zeros_like(v_acc)

        def one_tile(i, inner):
            at = pl.ds(pl.multiple_of(i * tile, tile), tile)
            query = q_buf[mine, at] * jnp.bfloat16(scale)
            grad = g_buf[mine, at]
            products = grad.astype(jnp.float32) * c_buf[mine, at].astype(jnp.float32)
            delta = jnp.sum(products.T, axis=1, keepdims=True)
            first = (((0,), (0,)), ((), ()))
            scores = lax.dot_general(query, keys, first, preferred_element_type=jnp.float32)
            scores = jnp.where(member, scores, -jnp.inf)
            exps = jnp.exp(scores - jnp.max(scores, axis=1, keepdims=True))
            probs = exps * (1.0 / jnp.sum(exps, axis=1, keepdims=True))
            v_acc[...] += jnp.dot(
                grad, probs.astype(jnp.bfloat16), preferred_element_type=jnp.float32
            )
            grad_probs = lax.dot_general(grad, values, first, preferred_element_type=jnp.float32)
            grad_scores = (probs * (grad_probs - delta)).astype(jnp.bfloat16)
            dq_buf[mine, at] = lax.dot_general(
                keys_scaled, grad_scores, (((1,), (1,)), ((), ())),
                preferred_element_type=jnp.float32,
            ).astype(jnp.bfloat16)
            k_acc[...] += jnp.dot(query, grad_scores, preferred_element_type=jnp.float32)
            return inner

        lax.fori_loop(0, length // tile, one_tile, 0)
        dk_buf[mine, :] = k_acc[...].astype(jnp.bfloat16)
        dv_buf[mine, :] = v_acc[...].astype(jnp.bfloat16)
        for t, (buf, out) in enumerate(outputs):
            pltpu.make_async_copy(
                buf.at[mine, cols(me)], out.at[0, head_rows(h, me), :], out_recv.at[t]
            ).start()

        def to_peer(k, inner):
            peer = (me + k) % n
            for t, (buf, out) in enumerate(outputs):
                pltpu.make_async_remote_copy(
                    src_ref=buf.at[mine, cols(peer)],
                    dst_ref=out.at[0, head_rows(h, me), :],
                    send_sem=out_send.at[t],
                    recv_sem=out_recv.at[t],
                    device_id={"seq": peer},
                    device_id_type=MESH,
                ).start()
            return inner

        lax.fori_loop(1, n, to_peer, 0)
        return carry

    lax.fori_loop(0, heads, one_head, 0)

    width = min(256, features)

    def weight_part(i, carry):
        at = pl.ds(pl.multiple_of(i * width, width), width)
        gw[:, at] = lax.dot_general(
            c_buf[...], cot[at, :], (((1,), (1,)), ((), ())), preferred_element_type=jnp.float32
        )
        return carry

    lax.fori_loop(0, features // width, weight_part, 0)
    swap = pltpu.make_async_remote_copy(
        src_ref=gw.at[pl.ds(pl.multiple_of((1 - rep) * half, half), half), :],
        dst_ref=gw_in,
        send_sem=gw_send,
        recv_sem=gw_recv,
        device_id={"rep": 1 - rep},
        device_id_type=MESH,
    )
    swap.start()
    swap.wait()
    gw_out[...] = gw[pl.ds(pl.multiple_of(rep * half, half), half), :] + gw_in[...]

    for step in range(nz):
        ag_step(step, arrived=False, send=False)
    others = (n - 1) * rows
    for t, (ref, _) in enumerate(inputs):
        gone = ref.at[0, pl.ds(0, others), :]
        pltpu.make_async_copy(gone, gone, in_send.at[t]).wait()
    gone = m_buf.at[:, pl.ds(0, (n - 1) * cells)]
    pltpu.make_async_copy(gone, gone, m_send).wait()
    for t, (buf, out) in enumerate(outputs):
        gone = buf.at[:, pl.ds(0, (n - 1) * cells)]
        pltpu.make_async_copy(gone, gone, out_send.at[t]).wait()
        pltpu.make_async_copy(out, out, out_recv.at[t]).wait()


def on_device(n, queries, key_vectors, value_vectors, context, cotangent, out_weight, membership):
    ny = 2 if n == 8 else 1
    nz = n // ny
    features, cells = queries.shape[1], queries.shape[2]
    rows, length = features // n, cells * n
    heads = rows // DH
    low = jnp.bfloat16
    dma = pltpu.SemaphoreType.DMA
    anywhere = pl.BlockSpec(memory_space=pl.ANY)
    return pl.pallas_call(
        functools.partial(kernel, n, ny),
        out_shape=(
            jax.ShapeDtypeStruct(queries.shape, low),
            jax.ShapeDtypeStruct(queries.shape, low),
            jax.ShapeDtypeStruct(queries.shape, low),
            jax.ShapeDtypeStruct((rows // 2, features), jnp.float32),
        ),
        in_specs=[anywhere] * 7,
        out_specs=(anywhere, anywhere, anywhere, pl.BlockSpec(memory_space=pltpu.VMEM)),
        scratch_shapes=[pltpu.VMEM((rows, length), low)] * 8
        + [
            pltpu.VMEM((features, length), low),
            pltpu.VMEM((rows, features), low),
            pltpu.VMEM((1, length), jnp.int32),
            pltpu.VMEM((rows, features), jnp.float32),
            pltpu.VMEM((rows // 2, features), jnp.float32),
            pltpu.VMEM((DH, length), jnp.float32),
            pltpu.VMEM((DH, length), jnp.float32),
            dma, dma, dma, dma,
            dma((4,)), dma((4, heads)),
            dma((4, nz, CHUNKS)), dma((CHUNKS, n)),
            dma((3,)), dma((3,)),
            dma, dma,
        ],
        compiler_params=pltpu.CompilerParams(
            collective_id=0, has_side_effects=True, vmem_limit_bytes=56 << 20
        ),
    )(queries, key_vectors, value_vectors, context, cotangent, out_weight, membership)


def solution(mesh):
    cellwise = P(("grp", "rep"), None, "seq")
    return jax.shard_map(
        functools.partial(on_device, mesh.shape["seq"]),
        mesh=mesh,
        in_specs=(cellwise,) * 5 + (P("grp", None), P(("grp", "rep"), "seq")),
        out_specs=(cellwise, cellwise, cellwise, P(("grp", "seq", "rep"), None)),
        check_vma=False,
    )
```

time: 288 us -> 120 us (0.42)
  Pallas kernels: 0 us -> 111 us
  blocking collectives: 104 us -> 0 us
  waiting for transfers between devices: 70 us -> 0 us
  matrix products: 45.7 us -> 0 us
  starting transfers between devices: 23.3 us -> 0 us
  local copies, waits for them, and re-layouts: 27 us -> 7.9 us
  between operations: 14.2 us -> 0.64 us
    pallas_call x0 -> x1, Pallas kernels: none -> 111 us  [on_device(): pl.pallas_call(functools.partial(kernel, n, ny), out_shape=(jax.ShapeDtyp...]
    all_to_all x3 -> x0, blocking collectives: 72.4 us -> none  [the longest x1 33.3 us: on_device(): lax.all_to_all(value_local, 'seq', split_axis=0, concat_axis=1, tiled=True)]
    all_to_all x5 -> x0, waiting for transfers between devices: 70 us -> none  [the longest x1 22.3 us: on_device(): lax.all_to_all(query_grads.reshape(head_count * DH, length), 'seq', split...]
    dot_general x10 -> x0, matrix products: 36.1 us -> none  [the longest x2 11.5 us: one_block(): jnp.einsum('hdq,hqk->hdk', grad_block, probs_low, preferred_element_type=...]
    all_gather x1 -> x0, blocking collectives: 32 us -> none  [on_device(): flags_all = lax.all_gather(membership, 'seq', axis=1, tiled=True)[0]]
    all_to_all x5 -> x0, starting transfers between devices: 23.3 us -> none  [the longest x1 8.31 us: on_device(): lax.all_to_all(query_grads.reshape(head_count * DH, length), 'seq', split...]
    all_to_all x8 -> x0, local copies, waits for them, and re-layouts: 10.4 us -> none  [the longest x1 2.18 us: on_device(): lax.all_to_all(value_local, 'seq', split_axis=0, concat_axis=1, tiled=True)]
    sub x2 -> x0, matrix products: 9.62 us -> none  [one_block(): exp_scores = jnp.exp(scores - highest)]
  transfers between devices with their start and end apart: 6 -> 0, of which waited for: 4 -> 0; matrix products, arithmetic and copies ran while one was open for 21% -> 0% of each run, Pallas kernels for 0% -> 0%
where the time goes in v1:
time: 120 us; the launch traced here: 119 us
  Pallas kernels  111 us (92%)
  local copies, waits for them, and re-layouts  7.9 us (7%)
    pallas_call x1, Pallas kernels, on_device(): pl.pallas_call(functools.partial(kernel, n, ny), out_shape=(jax.ShapeDtyp...  111 us
    unnamed x4, local copies, waits for them, and re-layouts  7.9 us

profile of v1, /device:TPU:0, one launch (start us, length us, event | category | flops | bytes accessed | tf_op | source)
XLA Modules:
  0.0 119.5 jit_solution(1439143726529700839)
XLA Ops:
  0.6 111.0 %shard_map.102 = (bf16[1,2048,128]{2,1,0:T(8,128)(2,1)}, bf16[1,2048,128]{2,1,0:T(8,128)(2,1)}, bf16[1,2048,128]{2,1,0:T(8,128)(2,1)}, f32[128,2048]{1,0:T(8,128)}) custom-call(bf16[1,2048,128]{2,1,0:T(8,128)(2,1)} %refs_0_.1, bf16[1,2048,128]{2,1,0:T(8,128)(2,1)} %refs_1_.1, bf16[1,2048,128]{2,1,0:T(8,128)(2,1)} %refs_2_.1, bf16[1,2048,128]{2,1,0:T(8,128)(2,1)} %refs_3_.1, ...), custom_call_target="tpu_custom_call" | custom-call | tf_op jit(solution)/shard_map/pallas_call | solution.py:280
  111.6 1.9 %copy.15 = bf16[1,2048,128]{2,1,0:T(8,128)(2,1)} copy(bf16[1,2048,128]{2,1,0:T(8,128)(2,1)} %get-tuple-element.8) | data formatting | bytes 1048576
  113.5 1.9 %copy.16 = bf16[1,2048,128]{2,1,0:T(8,128)(2,1)} copy(bf16[1,2048,128]{2,1,0:T(8,128)(2,1)} %get-tuple-element.9) | data formatting | bytes 1048576
  115.3 1.9 %copy.17 = bf16[1,2048,128]{2,1,0:T(8,128)(2,1)} copy(bf16[1,2048,128]{2,1,0:T(8,128)(2,1)} %get-tuple-element.10) | data formatting | bytes 1048576
  117.2 2.3 %copy.18 = f32[128,2048]{1,0:T(8,128)} copy(f32[128,2048]{1,0:T(8,128)} %get-tuple-element.11) | data formatting | bytes 2097152

commit v2 on v1

--- a/solution.py
+++ b/solution.py
@@ -10,7 +10,7 @@
 
 DH = 64
 MESH = pl.DeviceIdType.MESH
-CHUNKS = 2
+CHUNKS = 4
 
 
 def kernel(n, ny, *refs):
@@ -19,7 +19,7 @@
      q_buf, k_buf, v_buf, c_buf, g_buf, dq_buf, dk_buf, dv_buf,
      cot, w_buf, m_buf, gw, gw_in, k_acc, v_acc,
      w_sem, own_sem, m_send, m_recv, in_send, in_recv,
-     ag_send, ag_recv, out_send, out_recv, gw_send, gw_recv) = refs
+     ag_send, ag_recv, out_send, out_recv, gw_send, gw_recv, gw_sem) = refs
     me = lax.axis_index("seq")
     rep = lax.axis_index("rep")
     nz = n // ny
@@ -109,14 +109,16 @@
                 if step > 0:
                     cross(down * ny + y, 3)
 
-    def send_inputs(h):
+    def keep_inputs(h, carry):
         for t, (ref, buf) in enumerate(inputs):
             pltpu.make_async_copy(
                 ref.at[0, head_rows(h, me), :], buf.at[head_rows(h), cols(me)], in_recv.at[t, h]
             ).start()
-
+        return carry
+
+    def send_inputs(h, column, first):
         def to_peer(k, carry):
-            peer = (me + k) % n
+            peer = (z + k) % nz * ny + column
             for t, (ref, buf) in enumerate(inputs):
                 pltpu.make_async_remote_copy(
                     src_ref=ref.at[0, head_rows(h, peer), :],
@@ -128,7 +130,7 @@
                 ).start()
             return carry
 
-        lax.fori_loop(1, n, to_peer, 0)
+        lax.fori_loop(first, nz, to_peer, 0)
 
     def send_members(k, carry):
         pltpu.make_async_remote_copy(
@@ -146,10 +148,15 @@
         ag_step(step, arrived=step > 0, send=True)
         if step == 0:
             lax.fori_loop(1, n, send_members, 0)
+            lax.fori_loop(0, heads, keep_inputs, 0)
         upto = -(-(step + 1) * heads // nz)
         for h in range(sent, upto):
-            send_inputs(h)
+            send_inputs(h, y, 1)
+            if ny == 2 and h > 0:
+                send_inputs(h - 1, 1 - y, 0)
         sent = upto
+    if ny == 2:
+        send_inputs(heads - 1, 1 - y, 0)
     if ny == 2:
         for origin_z in range(nz):
             for part in range(CHUNKS):
@@ -252,7 +259,9 @@
     )
     swap.start()
     swap.wait()
-    gw_out[...] = gw[pl.ds(pl.multiple_of(rep * half, half), half), :] + gw_in[...]
+    gw_in[...] += gw[pl.ds(pl.multiple_of(rep * half, half), half), :]
+    total = pltpu.make_async_copy(gw_in, gw_out, gw_sem)
+    total.start()
 
     for step in range(nz):
         ag_step(step, arrived=False, send=False)
@@ -266,6 +275,22 @@
         gone = buf.at[:, pl.ds(0, (n - 1) * cells)]
         pltpu.make_async_copy(gone, gone, out_send.at[t]).wait()
         pltpu.make_async_copy(out, out, out_recv.at[t]).wait()
+    total.wait()
+
+
+def hand_over(*refs):
+    sources, targets, stages, (sem_in, sem_out) = refs[:4], refs[4:8], refs[8:12], refs[12:]
+    reads, writes = [], []
+    for t in range(4):
+        reads.append(pltpu.make_async_copy(sources[t], stages[t], sem_in.at[t]))
+        writes.append(pltpu.make_async_copy(stages[t], targets[t], sem_out.at[t]))
+    for copy in reads:
+        copy.start()
+    for read, write in zip(reads, writes):
+        read.wait()
+        write.start()
+    for copy in writes:
+        copy.wait()
 
 
 def on_device(n, queries, key_vectors, value_vectors, context, cotangent, out_weight, membership):
@@ -277,7 +302,7 @@
     low = jnp.bfloat16
     dma = pltpu.SemaphoreType.DMA
     anywhere = pl.BlockSpec(memory_space=pl.ANY)
-    return pl.pallas_call(
+    parts = pl.pallas_call(
         functools.partial(kernel, n, ny),
         out_shape=(
             jax.ShapeDtypeStruct(queries.shape, low),
@@ -286,7 +311,7 @@
             jax.ShapeDtypeStruct((rows // 2, features), jnp.float32),
         ),
         in_specs=[anywhere] * 7,
-        out_specs=(anywhere, anywhere, anywhere, pl.BlockSpec(memory_space=pltpu.VMEM)),
+        out_specs=(anywhere,) * 4,
         scratch_shapes=[pltpu.VMEM((rows, length), low)] * 8
         + [
             pltpu.VMEM((features, length), low),
@@ -300,12 +325,20 @@
             dma((4,)), dma((4, heads)),
             dma((4, nz, CHUNKS)), dma((CHUNKS, n)),
             dma((3,)), dma((3,)),
-            dma, dma,
+            dma, dma, dma,
         ],
         compiler_params=pltpu.CompilerParams(
             collective_id=0, has_side_effects=True, vmem_limit_bytes=56 << 20
         ),
     )(queries, key_vectors, value_vectors, context, cotangent, out_weight, membership)
+    return pl.pallas_call(
+        hand_over,
+        out_shape=tuple(jax.ShapeDtypeStruct(part.shape, part.dtype) for part in parts),
+        in_specs=[anywhere] * 4,
+        out_specs=(anywhere,) * 4,
+        scratch_shapes=[pltpu.VMEM(part.shape, part.dtype) for part in parts]
+        + [dma((4,)), dma((4,))],
+    )(*parts)
 
 
 def solution(mesh):

time: 120 us -> 112 us (0.933)
  local copies, waits for them, and re-layouts: 7.9 us -> 0 us
    unnamed x4 -> x0, local copies, waits for them, and re-layouts: 7.9 us -> none
    pallas_call x1, Pallas kernels: 111 us -> 108 us  [on_device(): pl.pallas_call(functools.partial(kernel, n, ny), out_shape=(jax.ShapeDtyp...]
    pallas_call x0 -> x1, Pallas kernels: none -> 2.74 us  [on_device(): pl.pallas_call(hand_over, out_shape=tuple((jax.ShapeDtypeStruct(part.shap...]
where the time goes in v2:
time: 112 us; the launch traced here: 111 us
  Pallas kernels  111 us (99%)
    pallas_call x1, Pallas kernels, on_device(): pl.pallas_call(functools.partial(kernel, n, ny), out_shape=(jax.ShapeDtyp...  108 us
    pallas_call x1, Pallas kernels, on_device(): pl.pallas_call(hand_over, out_shape=tuple((jax.ShapeDtypeStruct(part.shap...  2.74 us

profile of v2, /device:TPU:0, one launch (start us, length us, event | category | flops | bytes accessed | tf_op | source)
XLA Modules:
  0.0 111.4 jit_solution(17898468190545929591)
XLA Ops:
  0.6 108.0 %shard_map.102 = (bf16[1,2048,128]{2,1,0:T(8,128)(2,1)}, bf16[1,2048,128]{2,1,0:T(8,128)(2,1)}, bf16[1,2048,128]{2,1,0:T(8,128)(2,1)}, f32[128,2048]{1,0:T(8,128)}) custom-call(bf16[1,2048,128]{2,1,0:T(8,128)(2,1)} %refs_0_.1, bf16[1,2048,128]{2,1,0:T(8,128)(2,1)} %refs_1_.1, bf16[1,2048,128]{2,1,0:T(8,128)(2,1)} %refs_2_.1, bf16[1,2048,128]{2,1,0:T(8,128)(2,1)} %refs_3_.1, ...), custom_call_target="tpu_custom_call" | custom-call | tf_op jit(solution)/shard_map/pallas_call | solution.py:305
  108.7 2.7 %shard_map.103 = (bf16[1,2048,128]{2,1,0:T(8,128)(2,1)}, bf16[1,2048,128]{2,1,0:T(8,128)(2,1)}, bf16[1,2048,128]{2,1,0:T(8,128)(2,1)}, f32[128,2048]{1,0:T(8,128)}) custom-call(bf16[1,2048,128]{2,1,0:T(8,128)(2,1)} %get-tuple-element.8.refs_0_, bf16[1,2048,128]{2,1,0:T(8,128)(2,1)} %get-tuple-element.9.refs_1_, ...), custom_call_target="tpu_custom_call" | custom-call | tf_op jit(solution)/shard_map/pallas_call | solution.py:334

commit v3 on v2

--- a/solution.py
+++ b/solution.py
@@ -149,14 +149,14 @@
         if step == 0:
             lax.fori_loop(1, n, send_members, 0)
             lax.fori_loop(0, heads, keep_inputs, 0)
-        upto = -(-(step + 1) * heads // nz)
+        upto = -(-step * heads // nz)
         for h in range(sent, upto):
-            send_inputs(h, y, 1)
-            if ny == 2 and h > 0:
-                send_inputs(h - 1, 1 - y, 0)
+            for column, first in ((y, 1), (1 - y, 0))[:ny]:
+                send_inputs(h, column, first)
         sent = upto
-    if ny == 2:
-        send_inputs(heads - 1, 1 - y, 0)
+    for h in range(sent, heads):
+        for column, first in ((y, 1), (1 - y, 0))[:ny]:
+            send_inputs(h, column, first)
     if ny == 2:
         for origin_z in range(nz):
             for part in range(CHUNKS):

time: 112 us -> 111 us (level)
  no operation moved by 1% of the time
where the time goes in v3:
time: 111 us
  Pallas kernels  111 us (100%)
    pallas_call x1, Pallas kernels, on_device(): pl.pallas_call(functools.partial(kernel, n, ny), out_shape=(jax.ShapeDtyp...  108 us
    pallas_call x1, Pallas kernels, on_device(): pl.pallas_call(hand_over, out_shape=tuple((jax.ShapeDtypeStruct(part.shap...  2.74 us

profile of v3, /device:TPU:0, one launch (start us, length us, event | category | flops | bytes accessed | tf_op | source)
XLA Modules:
  0.0 111.3 jit_solution(12015571269636866161)
XLA Ops:
  0.6 107.9 %shard_map.102 = (bf16[1,2048,128]{2,1,0:T(8,128)(2,1)}, bf16[1,2048,128]{2,1,0:T(8,128)(2,1)}, bf16[1,2048,128]{2,1,0:T(8,128)(2,1)}, f32[128,2048]{1,0:T(8,128)}) custom-call(bf16[1,2048,128]{2,1,0:T(8,128)(2,1)} %refs_0_.1, bf16[1,2048,128]{2,1,0:T(8,128)(2,1)} %refs_1_.1, bf16[1,2048,128]{2,1,0:T(8,128)(2,1)} %refs_2_.1, bf16[1,2048,128]{2,1,0:T(8,128)(2,1)} %refs_3_.1, ...), custom_call_target="tpu_custom_call" | custom-call | tf_op jit(solution)/shard_map/pallas_call | solution.py:305
  108.5 2.7 %shard_map.103 = (bf16[1,2048,128]{2,1,0:T(8,128)(2,1)}, bf16[1,2048,128]{2,1,0:T(8,128)(2,1)}, bf16[1,2048,128]{2,1,0:T(8,128)(2,1)}, f32[128,2048]{1,0:T(8,128)}) custom-call(bf16[1,2048,128]{2,1,0:T(8,128)(2,1)} %get-tuple-element.8.refs_0_, bf16[1,2048,128]{2,1,0:T(8,128)(2,1)} %get-tuple-element.9.refs_1_, ...), custom_call_target="tpu_custom_call" | custom-call | tf_op jit(solution)/shard_map/pallas_call | solution.py:334
